TPU v7x, 512 devices: a whole 4x8x8 slice. The times are simulated.
512 devices in a mesh: expert: 128 (over y, z, core), dp: 4 (over x).
Axes of the slice: x: 4, y: 8, z: 8, core: 2. Of those that a mesh axis runs over, the one named last changes fastest.
Arguments:
- hidden: bfloat16 [128, 4, 256, 1024], P('expert', 'dp'), may hold values from -6 to 6
- w_down: bfloat16 [128, 1024, 3584], P('expert', 'dp'), may hold values from -0.1875 to 0.1875
- expert_ids: int32 [4, 2048, 8], P('dp', 'expert'), may hold values from 0 to 127, all different within a row; in each aligned block of 16 rows (0 to 15, 16 to 31, ..., all dimensions but the last counted through in order) at most 2 rows name the same one
- route_weights: float32 [4, 2048, 8], P('dp', 'expert'), may hold values from 0.1 to 0.6
- grad_out: bfloat16 [4, 2048, 3584], P('dp', 'expert'), may hold values from -6 to 6
Outputs:
- mixed: bfloat16 [4, 2048, 3584], P('dp', 'expert')
- d_hidden: bfloat16 [128, 4, 256, 1024], P('expert', 'dp')
- d_w_down: bfloat16 [128, 1024, 3584], P('expert', 'dp')
- d_route: float32 [4, 2048, 8], P('dp', 'expert')
Inputs may be any that keep to these rules, and one draw needn't show every extreme that they name: `expert_ids`: among the 16 tokens of one device no expert is chosen more than 2 times, and some expert is chosen exactly 2 times; the 8 choices of a token are distinct.
All inputs are finite; a program needn't handle non-finite values.
Results may differ from a plain program's by a relative error of at most 0.0085.
Values may be sent and summed in bfloat16 or wider, within the bound.
A program may use at most 128 MiB of HBM per device.

v0:
```python
import jax
import jax.numpy as jnp
from jax import lax
from jax.sharding import PartitionSpec as P


def slot_ranks(choices, experts):
    flat = choices.reshape(-1)
    onehot = (flat[:, None] == jnp.arange(experts, dtype=jnp.int32)[None, :]).astype(jnp.int32)
    earlier = jnp.cumsum(onehot, axis=0) - onehot
    return jnp.sum(earlier * onehot, axis=1).reshape(choices.shape)


def on_device(hidden, w_down, expert_ids, route_weights, grad_out):
    experts = lax.axis_size("expert")
    groups = lax.axis_size("dp")
    slots = hidden.shape[2] // experts
    width = w_down.shape[2]
    w_whole = lax.all_gather(w_down, "dp", axis=1, tiled=True)[0]
    out_slots = jnp.dot(hidden[0, 0], w_whole, preferred_element_type=jnp.float32).astype(
        jnp.bfloat16
    )
    arrived = lax.all_to_all(
        out_slots.reshape(experts, slots, width), "expert", split_axis=0, concat_axis=0, tiled=True
    )
    arrived = arrived.reshape(experts * slots, width)
    choices = expert_ids[0]
    weights = route_weights[0]
    cotangent = grad_out[0].astype(jnp.float32)
    rows = choices * slots + slot_ranks(choices, experts)
    out_pair = arrived[rows].astype(jnp.float32)
    mixed = jnp.einsum("tk,tkd->td", weights, out_pair)
    d_route = jnp.einsum("td,tkd->tk", cotangent, out_pair)
    grad_pair = (weights[..., None] * cotangent[:, None, :]).astype(jnp.bfloat16)
    outgoing = jnp.zeros((experts * slots, width), jnp.bfloat16)
    outgoing = outgoing.at[rows.reshape(-1)].set(grad_pair.reshape(-1, width))
    mine = lax.all_to_all(
        outgoing.reshape(experts, 1, slots, width),
        "expert",
        split_axis=0,
        concat_axis=0,
        tiled=True,
    )
    own_grads = mine[:, 0]
    d_hidden = jnp.einsum(
        "rd,hd->rh", own_grads.reshape(-1, width), w_whole, preferred_element_type=jnp.float32
    ).astype(jnp.bfloat16)
    columns = lax.all_to_all(hidden, "dp", split_axis=3, concat_axis=1, tiled=True)[0]
    columns = columns.reshape(groups, experts, slots, columns.shape[-1])
    cw = width // 2
    parts = []
    for c in range(2):
        slot_grads = lax.all_gather(mine[..., c * cw : (c + 1) * cw], "dp", axis=1, tiled=True)
        parts.append(
            jnp.einsum(
                "gsch,sgcd->hd", columns, slot_grads, preferred_element_type=jnp.float32
            ).astype(jnp.bfloat16)
        )
    d_weight = jnp.concatenate(parts, axis=1)
    return (
        mixed.astype(jnp.bfloat16)[None],
        d_hidden.reshape(hidden.shape),
        d_weight[None],
        d_route[None],
    )


def solution(mesh):
    placed = (
        P("expert", "dp", None, None),
        P("expert", "dp", None),
        P("dp", "expert", None),
        P("dp", "expert", None),
        P("dp", "expert", None),
    )
    return jax.shard_map(
        on_device,
        mesh=mesh,
        in_specs=placed,
        out_specs=(
            P("dp", "expert", None),
            P("expert", "dp", None, None),
            P("expert", "dp", None),
            P("dp", "expert", None),
        ),
        check_vma=False,
    )
```

profile of v0, /device:TPU:1, one launch (start us, length us, event | category | flops | bytes accessed | tf_op | source)
XLA Modules:
  0.0 227.6 jit_solution(7683013739206800182)
XLA Ops:
  7.2 0.7 all-gather.4.cloned.1.call-update
  8.6 0.2 reduce_window_sum.11
  8.8 0.2 select_reduce_fusion
  9.0 2.5 %scatter_custom_fusion = bf16[256,3584]{1,0:T(8,128)(2,1)S(1)} fusion(s32[128]{0:T(128)S(1)} %fusion.33, f32[16,3584]{1,0:T(8,128)S(1)} %bitcast_convert_fusion.1, f32[128]{0:T(128)S(1)} %mul.53, bf16[]{:T(256)} %constant.7.clone.1), kind=kCustom, calls=%fused_computation.18 | custom fusion | flops 917504 | bytes 2064898 | tf_op jit(solution)/shard_map/scatter | solution.py:36
  11.5 1.6 reshape.99
  13.2 64.9 %all_to_all.25 = bf16[128,1,2,3584]{3,2,1,0:T(2,128)(2,1)S(1)} all-to-all(bf16[128,1,2,3584]{3,2,1,0:T(2,128)(2,1)} %bitcast.87), channel_id=1, replica_groups=mesh['expert'=128,'dp'=4] {'expert'}, dimensions={0} | all-to-all | bytes 3670016 | tf_op jit(solution)/shard_map/all_to_all | solution.py:37
  78.1 2.2 fusion.34
  80.2 3.6 %copy.71 = bf16[128,1,2,1792]{0,3,1,2:T(8,128)(2,1)} copy(bf16[128,1,2,1792]{3,2,1,0:T(2,128)(2,1)} %get-tuple-element.24) | data formatting | bytes 1835008
  83.9 2.1 copy.72
  86.0 0.9 copy.58
  86.9 0.5 broadcast.58
  87.4 3.8 %reduce = bf16[1024,256]{1,0:T(8,128)(2,1)S(1)} reduce(bf16[1024,1,1,256]{3,2,1,0:T(2,128)(2,1)S(1)} %bitcast.89, bf16[]{:T(256)} %broadcast.58), dimensions={1,2}, to_apply=%bitcast.78.reduce_sub_computation | reduce | bytes 1048578
  91.3 0.9 reshape.126
  92.2 4.0 %all-to-all-start.2 = ((bf16[4,2,32768]{2,1,0:T(2,128)(2,1)}), bf16[4,2,32768]{2,1,0:T(2,128)(2,1)S(1)}, u32[]{:S(2)}, u32[]{:S(2)}) async-start(bf16[4,2,32768]{2,1,0:T(2,128)(2,1)} %reshape.126), calls=%async_computation.2 | async-start | bytes 1048576 | tf_op jit(solution)/shard_map/all_to_all | solution.py:48
  96.2 6.4 %fusion.4 = bf16[256,3584]{1,0:T(8,128)(2,1)} fusion(bf16[1,1024,3584]{2,1,0:T(8,128)(2,1)} %all-gather.4.cloned.1.call-done, bf16[1,1,256,1024]{3,2,1,0:T(8,128)(2,1)S(1)} %copy-done.1), kind=kOutput, calls=%fused_computation.6 | convolution fusion | flops 1879965696 | bytes 9699328 | tf_op jit(solution)/shard_map/dot_general | solution.py:20
  102.6 4.8 %reshape.96 = bf16[128,2,3584]{2,1,0:T(2,128)(2,1)} reshape(bf16[256,3584]{1,0:T(8,128)(2,1)} %fusion.4) | data formatting | bytes 3670016 | tf_op jit(solution)/shard_map/reshape | solution.py:24
  107.3 15.9 %all-to-all-start = ((bf16[128,2,3584]{2,1,0:T(2,128)(2,1)}), bf16[128,2,3584]{2,1,0:T(2,128)(2,1)}, u32[]{:S(2)}, u32[]{:S(2)}) async-start(bf16[128,2,3584]{2,1,0:T(2,128)(2,1)} %reshape.96), calls=%async_computation | async-start | bytes 3670016 | tf_op jit(solution)/shard_map/all_to_all | solution.py:23
  123.6 0.5 reshape.127
  124.3 1.1 copy.59
  125.3 1.7 reshape_squeeze.6
  127.0 22.5 %all-gather.6.cloned.1.call-done = bf16[128,4,2,1792]{0,3,1,2:T(8,128)(2,1)} async-done(((bf16[128,1,2,1792]{0,3,1,2:T(8,128)(2,1)}), bf16[128,4,2,1792]{0,3,1,2:T(8,128)(2,1)}) %all-gather.6.cloned.1.call-update) | async-done | bytes 3670032 | tf_op jit(solution)/shard_map/all_gather | solution.py:53
  149.5 3.2 %fusion.10 = bf16[256,1792]{0,1:T(8,128)(2,1)S(1)} fusion(bf16[128,4,2,1792]{0,3,1,2:T(8,128)(2,1)} %all-gather.6.cloned.1.call-done, bf16[4,128,2,256]{3,0,2,1:T(4,128)(2,1)S(1)} %bitcast.91), kind=kOutput, calls=%fused_computation.12 | convolution fusion | flops 939982848 | bytes 5111808 | tf_op jit(solution)/shard_map/gsch,sgcd->hd/dot_general | solution.py:55
  152.7 48.4 %all-gather.8.cloned.1.call-done = bf16[128,4,2,1792]{0,3,1,2:T(8,128)(2,1)} async-done(((bf16[128,1,2,1792]{0,3,1,2:T(8,128)(2,1)}), bf16[128,4,2,1792]{0,3,1,2:T(8,128)(2,1)}) %all-gather.8.cloned.1.call-update) | async-done | bytes 3670032 | tf_op jit(solution)/shard_map/all_gather | solution.py:53
  201.1 3.2 %fusion.9 = bf16[256,1792]{0,1:T(8,128)(2,1)S(1)} fusion(bf16[128,4,2,1792]{0,3,1,2:T(8,128)(2,1)} %all-gather.8.cloned.1.call-done, bf16[4,128,2,256]{3,0,2,1:T(4,128)(2,1)S(1)} %bitcast.92), kind=kOutput, calls=%fused_computation.11 | convolution fusion | flops 939982848 | bytes 5111808 | tf_op jit(solution)/shard_map/gsch,sgcd->hd/dot_general | solution.py:55
  204.4 2.6 %copy.63 = bf16[1,256,3584]{2,1,0:T(8,128)(2,1)} copy(bf16[1,256,3584]{1,2,0:T(8,128)(2,1)S(1)} %maximum_bitcast_fusion) | data formatting | bytes 3670016
  207.0 6.5 %fusion.15 = bf16[1,1,256,1024]{3,2,1,0:T(8,128)(2,1)} fusion(bf16[256,3584]{1,0:T(8,128)(2,1)} %reshape_squeeze.6, bf16[1,1024,3584]{2,1,0:T(8,128)(2,1)} %all-gather.4.cloned.1.call-done), kind=kOutput, calls=%fused_computation.17 | convolution fusion | flops 1879310336 | bytes 9699328 | tf_op jit(solution)/shard_map/rd,hd->rh/dot_general | solution.py:45
  213.5 4.1 %reshape.97 = bf16[256,3584]{1,0:T(8,128)(2,1)S(1)} reshape(bf16[128,2,3584]{2,1,0:T(2,128)(2,1)} %all-to-all-done) | data formatting | bytes 3670016 | tf_op jit(solution)/shard_map/reshape | solution.py:26
  217.6 1.1 gather_fusion
  218.7 0.6 fusion.22
  219.3 0.4 fusion.20
  219.7 0.7 copy.82
  220.4 0.7 copy.69
  (39 shorter events, 1.4 us)
Async XLA Ops:
  7.2 0.8 copy-start.4
  7.2 1.1 copy-start.5
  7.2 1.8 copy-start.3
  7.2 89.0 %all-gather.4.cloned.1.call-start = ((), (), s32[]{:S(2)}) async-start(), calls=%async_computation.3 | async-start | bytes 9175040 | tf_op jit(solution)/shard_map/all_gather | solution.py:19
  7.9 141.6 %all-gather.6.cloned.1.call-start = ((), (), s32[]{:S(2)}) async-start(), calls=%async_computation.4 | async-start | bytes 4587520 | tf_op jit(solution)/shard_map/all_gather | solution.py:53
  83.8 2.2 copy-start
  83.8 117.3 %all-gather.8.cloned.1.call-start = ((), (), s32[]{:S(2)}) async-start(), calls=%async_computation.5 | async-start | bytes 4587520 | tf_op jit(solution)/shard_map/all_gather | solution.py:53
  91.3 4.9 %copy-start.1 = (bf16[1,1,256,1024]{3,2,1,0:T(8,128)(2,1)S(1)}, bf16[1,1,256,1024]{3,2,1,0:T(8,128)(2,1)}, u32[]{:S(2)}) copy-start(bf16[1,1,256,1024]{3,2,1,0:T(8,128)(2,1)} %param.5) | copy-start | bytes 1572868
  92.2 15.2 %all-to-all-start.2 = ((bf16[4,2,32768]{2,1,0:T(2,128)(2,1)}), bf16[4,2,32768]{2,1,0:T(2,128)(2,1)S(1)}, u32[]{:S(2)}, u32[]{:S(2)}) async-start(bf16[4,2,32768]{2,1,0:T(2,128)(2,1)} %reshape.126), calls=%async_computation.2 | async-start | bytes 1048576 | tf_op jit(solution)/shard_map/all_to_all | solution.py:48
  107.3 106.2 %all-to-all-start = ((bf16[128,2,3584]{2,1,0:T(2,128)(2,1)}), bf16[128,2,3584]{2,1,0:T(2,128)(2,1)}, u32[]{:S(2)}, u32[]{:S(2)}) async-start(bf16[128,2,3584]{2,1,0:T(2,128)(2,1)} %reshape.96), calls=%async_computation | async-start | bytes 3670016 | tf_op jit(solution)/shard_map/all_to_all | solution.py:23
  125.3 24.2 %copy-start.2 = (bf16[1,4,1,256,256]{4,1,3,2,0:T(4,128)(2,1)S(1)}, bf16[1,4,1,256,256]{4,1,3,2,0:T(4,128)(2,1)}, u32[]{:S(2)}) copy-start(bf16[1,4,1,256,256]{4,1,3,2,0:T(4,128)(2,1)} %copy.59) | copy-start | bytes 1572868
Sparse Core Ops, SparseCore 0:
  10.1 84.9 all-gather.3
  97.2 52.2 all-gather.5
  151.6 49.4 all-gather.7
where the time goes:
time: 228 us
  waiting for transfers between devices  71.7 us (31%)
  blocking collectives  64.9 us (28%)
  local copies, waits for them, and re-layouts  29.9 us (13%)
  matrix products  20.3 us (9%)
  starting transfers between devices  20 us (9%)
  between operations  14 us (6%)
  other arithmetic  6.95 us (3%)
    all_gather x2, waiting for transfers between devices, on_device(): lax.all_gather(mine[..., c * cw:(c + 1) * cw], 'dp', axis=1, tiled=True)  70.9 us
    all_to_all x1, blocking collectives, on_device(): lax.all_to_all(outgoing.reshape(experts, 1, slots, width), 'expert', spli...  64.9 us
    all_to_all x1, starting transfers between devices, on_device(): lax.all_to_all(out_slots.reshape(experts, slots, width), 'expert', split_...  15.9 us
    unnamed x22, local copies, waits for them, and re-layouts  11.3 us
    dot_general x1, matrix products, on_device(): jnp.einsum('rd,hd->rh', own_grads.reshape(-1, width), w_whole, preferred_...  6.53 us
    dot_general x1, matrix products, on_device(): jnp.dot(hidden[0, 0], w_whole, preferred_element_type=jnp.float32)  6.37 us
    dot_general x2, matrix products, on_device(): jnp.einsum('gsch,sgcd->hd', columns, slot_grads, preferred_element_type=j...  6.36 us
    reshape x1, local copies, waits for them, and re-layouts, on_device(): out_slots.reshape(experts, slots, width)  4.77 us
  transfers between devices with their start and end apart: 5, of which 2 were waited for; matrix products, arithmetic and copies ran while one was open for 22% of the time, Pallas kernels for 0%

commit v1 on v0

--- a/solution.py
+++ b/solution.py
@@ -2,6 +2,27 @@
 import jax.numpy as jnp
 from jax import lax
 from jax.sharding import PartitionSpec as P
+
+
+def ring_gather(value, axis, dim):
+    size, place, width = (lax.axis_size(axis), lax.axis_index(axis), value.shape[dim])
+    ahead = [(i, (i + 1) % size) for i in range(size)]
+    backward = [(i, (i - 1) % size) for i in range(size)]
+    out = jnp.zeros((*value.shape[:dim], size * width, *value.shape[dim + 1 :]), value.dtype)
+    out = lax.dynamic_update_slice_in_dim(out, value, place * width, axis=dim)
+    from_left = from_right = value
+    halfway = size // 2
+    for step in range(1, halfway + 1):
+        from_left = lax.ppermute(from_left, axis, ahead)
+        out = lax.dynamic_update_slice_in_dim(
+            out, from_left, (place - step) % size * width, axis=dim
+        )
+        if step < size - halfway:
+            from_right = lax.ppermute(from_right, axis, backward)
+            out = lax.dynamic_update_slice_in_dim(
+                out, from_right, (place + step) % size * width, axis=dim
+            )
+    return out
 
 
 def slot_ranks(choices, experts):
@@ -50,7 +71,7 @@
     cw = width // 2
     parts = []
     for c in range(2):
-        slot_grads = lax.all_gather(mine[..., c * cw : (c + 1) * cw], "dp", axis=1, tiled=True)
+        slot_grads = ring_gather(mine[..., c * cw : (c + 1) * cw], "dp", 1)
         parts.append(
             jnp.einsum(
                 "gsch,sgcd->hd", columns, slot_grads, preferred_element_type=jnp.float32

time: 228 us -> 220 us (0.965)
  blocking collectives: 64.9 us -> 0 us
  starting transfers between devices: 20 us -> 52.1 us
  local copies, waits for them, and re-layouts: 29.9 us -> 58 us
  matrix products: 20.3 us -> 17.3 us
    all_gather x2 -> x0, waiting for transfers between devices: 70.9 us -> none  [on_device(): lax.all_gather(mine[..., c * cw:(c + 1) * cw], 'dp', axis=1, tiled=True)]
    all_to_all x1 -> x0, blocking collectives: 64.9 us -> none  [on_device(): lax.all_to_all(outgoing.reshape(experts, 1, slots, width), 'expert', spli...]
    all_to_all x0 -> x1, waiting for transfers between devices: none -> 44.3 us  [on_device(): lax.all_to_all(outgoing.reshape(experts, 1, slots, width), 'expert', spli...]
    ppermute x0 -> x6, waiting for transfers between devices: none -> 23.4 us  [the longest x4 23.4 us: ring_gather(): from_left = lax.ppermute(from_left, axis, ahead)]
    all_to_all x0 -> x1, starting transfers between devices: none -> 20.4 us  [on_device(): lax.all_to_all(outgoing.reshape(experts, 1, slots, width), 'expert', spli...]
    ppermute x0 -> x6, local copies, waits for them, and re-layouts: none -> 17.7 us  [the longest x4 10.4 us: ring_gather(): from_left = lax.ppermute(from_left, axis, ahead)]
    ppermute x0 -> x6, starting transfers between devices: none -> 17.4 us  [the longest x2 9.06 us: ring_gather(): from_right = lax.ppermute(from_right, axis, backward)]
    dynamic_update_slice x0 -> x8, local copies, waits for them, and re-layouts: none -> 7.22 us  [the longest x4 4.04 us: ring_gather(): lax.dynamic_update_slice_in_dim(out, from_left, (place - step) % size * w...]
  transfers between devices with their start and end apart: 5 -> 10, of which waited for: 2 -> 4; matrix products, arithmetic and copies ran while one was open for 22% -> 33% of each run, Pallas kernels for 0% -> 0%
where the time goes in v1:
time: 220 us; the launch traced here: 219 us
  waiting for transfers between devices  70.2 us (32%)
  local copies, waits for them, and re-layouts  58 us (26%)
  starting transfers between devices  52.1 us (24%)
  matrix products  17.3 us (8%)
  between operations  14.4 us (7%)
  other arithmetic  6.96 us (3%)
    all_to_all x1, waiting for transfers between devices, on_device(): lax.all_to_all(outgoing.reshape(experts, 1, slots, width), 'expert', spli...  44.3 us
    ppermute x4, waiting for transfers between devices, ring_gather(): from_left = lax.ppermute(from_left, axis, ahead)  23.4 us
    all_to_all x1, starting transfers between devices, on_device(): lax.all_to_all(outgoing.reshape(experts, 1, slots, width), 'expert', spli...  20.4 us
    ppermute x4, local copies, waits for them, and re-layouts, ring_gather(): from_left = lax.ppermute(from_left, axis, ahead)  10.4 us
    all_to_all x1, starting transfers between devices, on_device(): lax.all_to_all(out_slots.reshape(experts, slots, width), 'expert', split_...  9.45 us
    unnamed x28, local copies, waits for them, and re-layouts  9.09 us
    ppermute x2, starting transfers between devices, ring_gather(): from_right = lax.ppermute(from_right, axis, backward)  9.06 us
    ppermute x4, starting transfers between devices, ring_gather(): from_left = lax.ppermute(from_left, axis, ahead)  8.3 us
  transfers between devices with their start and end apart: 10, of which 4 were waited for; matrix products, arithmetic and copies ran while one was open for 33% of the time, Pallas kernels for 0%

profile of v1, /device:TPU:1, one launch (start us, length us, event | category | flops | bytes accessed | tf_op | source)
XLA Modules:
  0.0 219.0 jit_solution(12615234433244323887)
XLA Ops:
  7.9 2.4 %copy.60 = bf16[1,1,256,1024]{2,1,0,3:T(2,128)(2,1)S(1)} copy(bf16[1,1,256,1024]{3,2,1,0:T(8,128)(2,1)} %param.5) | data formatting | bytes 1048576 | tf_op args[0]
  10.9 3.8 %reduce = bf16[1024,256]{1,0:T(8,128)(2,1)S(1)} reduce(bf16[1024,1,1,256]{3,2,1,0:T(2,128)(2,1)S(1)} %bitcast.88, bf16[]{:T(256)} %broadcast.65), dimensions={1,2}, to_apply=%bitcast.78.reduce_sub_computation | reduce | bytes 1048578
  15.6 4.8 %all-to-all-start.2 = ((bf16[4,2,32768]{2,1,0:T(2,128)(2,1)}), bf16[4,2,32768]{2,1,0:T(2,128)(2,1)S(1)}, u32[]{:S(2)}, u32[]{:S(2)}) async-start(bf16[4,2,32768]{2,1,0:T(2,128)(2,1)} %reshape.126), calls=%async_computation.2 | async-start | bytes 1048576 | tf_op jit(solution)/shard_map/all_to_all | solution.py:69
  21.4 2.5 %scatter_custom_fusion = bf16[256,3584]{1,0:T(8,128)(2,1)S(1)} fusion(s32[128]{0:T(128)S(1)} %fusion.33, f32[16,3584]{1,0:T(8,128)S(1)} %bitcast_convert_fusion.1, f32[128]{0:T(128)S(1)} %mul.53, bf16[]{:T(256)} %constant.46.clone.1), kind=kCustom, calls=%fused_computation.18 | custom fusion | flops 917504 | bytes 2064898 | tf_op jit(solution)/shard_map/scatter | solution.py:57
  25.6 1.7 all-to-all-done.2
  27.4 20.4 %all-to-all-start.1 = ((bf16[128,1,2,3584]{3,2,1,0:T(2,128)(2,1)}), bf16[128,1,2,3584]{3,2,1,0:T(2,128)(2,1)S(1)}, u32[]{:S(2)}, u32[]{:S(2)}) async-start(bf16[128,1,2,3584]{3,2,1,0:T(2,128)(2,1)} %bitcast.86), calls=%async_computation.1 | async-start | bytes 3670016 | tf_op jit(solution)/shard_map/all_to_all | solution.py:58
  49.9 44.3 %all-to-all-done.1 = bf16[128,1,2,3584]{3,2,1,0:T(2,128)(2,1)S(1)} async-done(((bf16[128,1,2,3584]{3,2,1,0:T(2,128)(2,1)}), bf16[128,1,2,3584]{3,2,1,0:T(2,128)(2,1)S(1)}, u32[]{:S(2)}, u32[]{:S(2)}) %all-to-all-start.1) | async-done | bytes 1835040 | tf_op jit(solution)/shard_map/all_to_all | solution.py:58
  94.3 2.2 fusion.34
  96.4 3.6 %copy.63 = bf16[128,1,2,1792]{0,3,1,2:T(8,128)(2,1)} copy(bf16[128,1,2,1792]{3,2,1,0:T(2,128)(2,1)} %get-tuple-element.21) | data formatting | bytes 1835008 | tf_op jit(solution)/shard_map/slice | solution.py:74
  100.0 2.3 %collective-permute-start.3 = (bf16[128,1,2,1792]{3,2,1,0:T(2,128)(2,1)}, bf16[128,1,2,1792]{3,2,1,0:T(2,128)(2,1)}, u32[]{:S(2)}, u32[]{:S(2)}) collective-permute-start(bf16[128,1,2,1792]{3,2,1,0:T(2,128)(2,1)} %get-tuple-element.21), channel_id=1, source_target_pairs={{0,1},{1,2},{2,3},{3,0},{4,5},{5,6},{6,7},{7,4},{8,9},{9,10},{10,1... | collective-permute-start | bytes 2752520 | tf_op jit(solution)/shard_map/ppermute | solution.py:16
  102.4 4.3 %collective-permute-start.4 = (bf16[128,1,2,1792]{3,2,1,0:T(2,128)(2,1)}, bf16[128,1,2,1792]{3,2,1,0:T(2,128)(2,1)}, u32[]{:S(2)}, u32[]{:S(2)}) collective-permute-start(bf16[128,1,2,1792]{3,2,1,0:T(2,128)(2,1)} %get-tuple-element.21), channel_id=1, source_target_pairs={{0,3},{1,0},{2,1},{3,2},{4,7},{5,4},{6,5},{7,6},{8,11},{9,8},{10,9... | collective-permute-start | bytes 2752520 | tf_op jit(solution)/shard_map/ppermute | solution.py:21
  106.7 1.9 collective-permute-start
  108.6 4.8 %collective-permute-start.1 = (bf16[128,1,2,1792]{3,2,1,0:T(2,128)(2,1)S(1)}, bf16[128,1,2,1792]{3,2,1,0:T(2,128)(2,1)}, u32[]{:S(2)}, u32[]{:S(2)}) collective-permute-start(bf16[128,1,2,1792]{3,2,1,0:T(2,128)(2,1)S(1)} %get-tuple-element.20), channel_id=1, source_target_pairs={{0,3},{1,0},{2,1},{3,2},{4,7},{5,4},{6,5},{7,6},{8,11},{9,8},{10,9... | collective-permute-start | bytes 2752520 | tf_op jit(solution)/shard_map/ppermute | solution.py:21
  113.4 2.4 %broadcast.59.clone = bf16[128,4,2,1792]{0,3,1,2:T(8,128)(2,1)} broadcast(bf16[]{:T(256)} %constant.46.clone.1), dimensions={} | broadcast | bytes 3670018 | tf_op jit(solution)/shard_map/broadcast.1
  116.8 2.1 copy.56
  120.5 5.3 %fusion.4 = bf16[256,3584]{1,0:T(8,128)(2,1)S(1)} fusion(bf16[1,1024,3584]{2,1,0:T(8,128)(2,1)} %all-gather.2.cloned.1.call-done, bf16[1,1,256,1024]{3,2,1,0:T(8,128)(2,1)} %param.5), kind=kOutput, calls=%fused_computation.6 | convolution fusion | flops 1879965696 | bytes 9699328 | tf_op jit(solution)/shard_map/dot_general | solution.py:41
  127.6 9.4 %all-to-all-start = ((bf16[128,2,3584]{2,1,0:T(2,128)(2,1)}), bf16[128,2,3584]{2,1,0:T(2,128)(2,1)}, u32[]{:S(2)}, u32[]{:S(2)}) async-start(bf16[128,2,3584]{2,1,0:T(2,128)(2,1)} %reshape.96), calls=%async_computation | async-start | bytes 3670016 | tf_op jit(solution)/shard_map/all_to_all | solution.py:44
  137.6 1.9 copy-done.4
  139.5 2.6 %copy.64 = bf16[128,1,2,1792]{0,3,1,2:T(8,128)(2,1)S(1)} copy(bf16[128,1,2,1792]{3,2,1,0:T(2,128)(2,1)} %collective-permute-done.3) | data formatting | bytes 1835008 | tf_op jit(solution)/shard_map/ppermute | solution.py:16
  142.2 1.9 collective-permute-start.5
  144.1 2.6 %copy.57 = bf16[128,1,2,1792]{0,3,1,2:T(8,128)(2,1)S(1)} copy(bf16[128,1,2,1792]{3,2,1,0:T(2,128)(2,1)} %collective-permute-done) | data formatting | bytes 1835008 | tf_op jit(solution)/shard_map/ppermute | solution.py:16
  146.7 2.1 collective-permute-start.2
  148.9 3.6 %copy.65 = bf16[128,1,2,1792]{0,3,1,2:T(8,128)(2,1)} copy(bf16[128,1,2,1792]{3,2,1,0:T(2,128)(2,1)} %collective-permute-done.4) | data formatting | bytes 1835008 | tf_op jit(solution)/shard_map/ppermute | solution.py:21
  152.5 3.7 %copy.58 = bf16[128,1,2,1792]{0,3,1,2:T(8,128)(2,1)} copy(bf16[128,1,2,1792]{3,2,1,0:T(2,128)(2,1)} %collective-permute-done.1) | data formatting | bytes 1835008 | tf_op jit(solution)/shard_map/ppermute | solution.py:21
  160.2 6.3 %collective-permute-done.5 = bf16[128,1,2,1792]{3,2,1,0:T(2,128)(2,1)} collective-permute-done((bf16[128,1,2,1792]{3,2,1,0:T(2,128)(2,1)}, bf16[128,1,2,1792]{3,2,1,0:T(2,128)(2,1)}, u32[]{:S(2)}, u32[]{:S(2)}) %collective-permute-start.5) | collective-permute-done | bytes 917536 | tf_op jit(solution)/shard_map/ppermute | solution.py:16
  166.5 2.6 %copy.66 = bf16[128,1,2,1792]{0,3,1,2:T(8,128)(2,1)S(1)} copy(bf16[128,1,2,1792]{3,2,1,0:T(2,128)(2,1)} %collective-permute-done.5) | data formatting | bytes 1835008 | tf_op jit(solution)/shard_map/ppermute | solution.py:16
  169.1 17.0 %collective-permute-done.2 = bf16[128,1,2,1792]{3,2,1,0:T(2,128)(2,1)} collective-permute-done((bf16[128,1,2,1792]{3,2,1,0:T(2,128)(2,1)}, bf16[128,1,2,1792]{3,2,1,0:T(2,128)(2,1)}, u32[]{:S(2)}, u32[]{:S(2)}) %collective-permute-start.2) | collective-permute-done | bytes 917536 | tf_op jit(solution)/shard_map/ppermute | solution.py:16
  186.2 2.6 %copy.59 = bf16[128,1,2,1792]{0,3,1,2:T(8,128)(2,1)S(1)} copy(bf16[128,1,2,1792]{3,2,1,0:T(2,128)(2,1)} %collective-permute-done.2) | data formatting | bytes 1835008 | tf_op jit(solution)/shard_map/ppermute | solution.py:16
  190.9 3.3 %fusion.9 = bf16[256,1792]{0,1:T(8,128)(2,1)S(1)} fusion(bf16[128,4,2,1792]{0,3,1,2:T(8,128)(2,1)} %constant_dynamic-update-slice_fusion.7, bf16[4,128,2,256]{3,0,2,1:T(4,128)(2,1)S(1)} %bitcast.90), kind=kOutput, calls=%fused_computation.11 | convolution fusion | flops 939982848 | bytes 5111808 | tf_op jit(solution)/shard_map/gsch,sgcd->hd/dot_general | solution.py:76
  195.5 2.6 %copy.68 = bf16[1,256,3584]{2,1,0:T(8,128)(2,1)} copy(bf16[1,256,3584]{1,2,0:T(8,128)(2,1)S(1)} %maximum_bitcast_fusion) | data formatting | bytes 3670016
  198.1 6.5 %fusion.15 = bf16[1,1,256,1024]{3,2,1,0:T(8,128)(2,1)} fusion(bf16[256,3584]{1,0:T(8,128)(2,1)} %reshape_squeeze.6, bf16[1,1024,3584]{2,1,0:T(8,128)(2,1)} %all-gather.2.cloned.1.call-done), kind=kOutput, calls=%fused_computation.17 | convolution fusion | flops 1879310336 | bytes 9699328 | tf_op jit(solution)/shard_map/rd,hd->rh/dot_general | solution.py:66
  204.6 4.1 %reshape.97 = bf16[256,3584]{1,0:T(8,128)(2,1)S(1)} reshape(bf16[128,2,3584]{2,1,0:T(2,128)(2,1)} %all-to-all-done) | data formatting | bytes 3670016 | tf_op jit(solution)/shard_map/reshape | solution.py:47
  (70 shorter events, 22.6 us)
Async XLA Ops:
  7.2 13.3 %copy-start.8 = (s32[1,16,8]{1,2,0:T(8,128)S(1)}, s32[1,16,8]{1,2,0:T(8,128)}, u32[]{:S(2)}) copy-start(s32[1,16,8]{1,2,0:T(8,128)} %param.7) | copy-start | bytes 1540
  7.2 13.5 %copy-start.7 = (bf16[1,16,3584]{2,1,0:T(8,128)(2,1)S(1)}, bf16[1,16,3584]{2,1,0:T(8,128)(2,1)}, u32[]{:S(2)}) copy-start(bf16[1,16,3584]{2,1,0:T(8,128)(2,1)} %param.9) | copy-start | bytes 344068
  7.2 13.7 %copy-start.9 = (f32[1,16,8]{1,2,0:T(8,128)S(1)}, f32[1,16,8]{1,2,0:T(8,128)}, u32[]{:S(2)}) copy-start(f32[1,16,8]{1,2,0:T(8,128)} %param.8) | copy-start | bytes 1540
  7.2 113.3 %all-gather.2.cloned.1.call-start = ((), (), s32[]{:S(2)}) async-start(), calls=%async_computation.3 | async-start | bytes 9175040 | tf_op jit(solution)/shard_map/all_gather | solution.py:40
  15.6 11.8 %all-to-all-start.2 = ((bf16[4,2,32768]{2,1,0:T(2,128)(2,1)}), bf16[4,2,32768]{2,1,0:T(2,128)(2,1)S(1)}, u32[]{:S(2)}, u32[]{:S(2)}) async-start(bf16[4,2,32768]{2,1,0:T(2,128)(2,1)} %reshape.126), calls=%async_computation.2 | async-start | bytes 1048576 | tf_op jit(solution)/shard_map/all_to_all | solution.py:69
  27.4 66.9 %all-to-all-start.1 = ((bf16[128,1,2,3584]{3,2,1,0:T(2,128)(2,1)}), bf16[128,1,2,3584]{3,2,1,0:T(2,128)(2,1)S(1)}, u32[]{:S(2)}, u32[]{:S(2)}) async-start(bf16[128,1,2,3584]{3,2,1,0:T(2,128)(2,1)} %bitcast.86), calls=%async_computation.1 | async-start | bytes 3670016 | tf_op jit(solution)/shard_map/all_to_all | solution.py:58
  100.0 15.7 %copy-start = (bf16[128,1,2,1792]{0,3,1,2:T(8,128)(2,1)S(1)}, bf16[128,1,2,1792]{0,3,1,2:T(8,128)(2,1)}, u32[]{:S(2)}) copy-start(bf16[128,1,2,1792]{0,3,1,2:T(8,128)(2,1)} %copy.63) | copy-start | bytes 2752516
  100.0 39.5 %collective-permute-start.3 = (bf16[128,1,2,1792]{3,2,1,0:T(2,128)(2,1)}, bf16[128,1,2,1792]{3,2,1,0:T(2,128)(2,1)}, u32[]{:S(2)}, u32[]{:S(2)}) collective-permute-start(bf16[128,1,2,1792]{3,2,1,0:T(2,128)(2,1)} %get-tuple-element.21), channel_id=1, source_target_pairs={{0,1},{1,2},{2,3},{3,0},{4,5},{5,6},{6,7},{7,4},{8,9},{9,10},{10,1... | collective-permute-start | bytes 2752520 | tf_op jit(solution)/shard_map/ppermute | solution.py:16
  102.4 46.5 %collective-permute-start.4 = (bf16[128,1,2,1792]{3,2,1,0:T(2,128)(2,1)}, bf16[128,1,2,1792]{3,2,1,0:T(2,128)(2,1)}, u32[]{:S(2)}, u32[]{:S(2)}) collective-permute-start(bf16[128,1,2,1792]{3,2,1,0:T(2,128)(2,1)} %get-tuple-element.21), channel_id=1, source_target_pairs={{0,3},{1,0},{2,1},{3,2},{4,7},{5,4},{6,5},{7,6},{8,11},{9,8},{10,9... | collective-permute-start | bytes 2752520 | tf_op jit(solution)/shard_map/ppermute | solution.py:21
  106.7 37.4 %collective-permute-start = (bf16[128,1,2,1792]{3,2,1,0:T(2,128)(2,1)S(1)}, bf16[128,1,2,1792]{3,2,1,0:T(2,128)(2,1)}, u32[]{:S(2)}, u32[]{:S(2)}) collective-permute-start(bf16[128,1,2,1792]{3,2,1,0:T(2,128)(2,1)S(1)} %get-tuple-element.20), channel_id=1, source_target_pairs={{0,1},{1,2},{2,3},{3,0},{4,5},{5,6},{6,7},{7,4},{8,9},{9,10},{10,1... | collective-permute-start | bytes 2752520 | tf_op jit(solution)/shard_map/ppermute | solution.py:16
  108.6 43.9 %collective-permute-start.1 = (bf16[128,1,2,1792]{3,2,1,0:T(2,128)(2,1)S(1)}, bf16[128,1,2,1792]{3,2,1,0:T(2,128)(2,1)}, u32[]{:S(2)}, u32[]{:S(2)}) collective-permute-start(bf16[128,1,2,1792]{3,2,1,0:T(2,128)(2,1)S(1)} %get-tuple-element.20), channel_id=1, source_target_pairs={{0,3},{1,0},{2,1},{3,2},{4,7},{5,4},{6,5},{7,6},{8,11},{9,8},{10,9... | collective-permute-start | bytes 2752520 | tf_op jit(solution)/shard_map/ppermute | solution.py:21
  127.6 9.9 %copy-start.1 = (bf16[128,1,2,1792]{0,3,1,2:T(8,128)(2,1)S(1)}, bf16[128,1,2,1792]{0,3,1,2:T(8,128)(2,1)}, u32[]{:S(2)}) copy-start(bf16[128,1,2,1792]{0,3,1,2:T(8,128)(2,1)} %copy.56) | copy-start | bytes 2752516
  127.6 77.0 %all-to-all-start = ((bf16[128,2,3584]{2,1,0:T(2,128)(2,1)}), bf16[128,2,3584]{2,1,0:T(2,128)(2,1)}, u32[]{:S(2)}, u32[]{:S(2)}) async-start(bf16[128,2,3584]{2,1,0:T(2,128)(2,1)} %reshape.96), calls=%async_computation | async-start | bytes 3670016 | tf_op jit(solution)/shard_map/all_to_all | solution.py:44
  137.6 1.9 copy-start.4
  142.2 24.4 %collective-permute-start.5 = (bf16[128,1,2,1792]{3,2,1,0:T(2,128)(2,1)}, bf16[128,1,2,1792]{3,2,1,0:T(2,128)(2,1)}, u32[]{:S(2)}, u32[]{:S(2)}) collective-permute-start(bf16[128,1,2,1792]{3,2,1,0:T(2,128)(2,1)} %collective-permute-done.3), channel_id=1, source_target_pairs={{0,1},{1,2},{2,3},{3,0},{4,5},{5,6},{6,7},{7,4},{8,9},{9,10},{10,1... | collective-permute-start | bytes 2752520 | tf_op jit(solution)/shard_map/ppermute | solution.py:16
  146.7 39.5 %collective-permute-start.2 = (bf16[128,1,2,1792]{3,2,1,0:T(2,128)(2,1)}, bf16[128,1,2,1792]{3,2,1,0:T(2,128)(2,1)}, u32[]{:S(2)}, u32[]{:S(2)}) collective-permute-start(bf16[128,1,2,1792]{3,2,1,0:T(2,128)(2,1)} %collective-permute-done), channel_id=1, source_target_pairs={{0,1},{1,2},{2,3},{3,0},{4,5},{5,6},{6,7},{7,4},{8,9},{9,10},{10,1... | collective-permute-start | bytes 2752520 | tf_op jit(solution)/shard_map/ppermute | solution.py:16
  152.5 5.7 %copy-start.2 = (bf16[128,1,2,1792]{0,3,1,2:T(8,128)(2,1)S(1)}, bf16[128,1,2,1792]{0,3,1,2:T(8,128)(2,1)}, u32[]{:S(2)}) copy-start(bf16[128,1,2,1792]{0,3,1,2:T(8,128)(2,1)} %copy.65) | copy-start | bytes 2752516
  156.1 3.0 %copy-start.3 = (bf16[128,1,2,1792]{0,3,1,2:T(8,128)(2,1)S(1)}, bf16[128,1,2,1792]{0,3,1,2:T(8,128)(2,1)}, u32[]{:S(2)}) copy-start(bf16[128,1,2,1792]{0,3,1,2:T(8,128)(2,1)} %copy.58) | copy-start | bytes 2752516
  160.2 30.7 %copy-start.6 = (bf16[1,4,1,256,256]{4,1,3,2,0:T(4,128)(2,1)S(1)}, bf16[1,4,1,256,256]{4,1,3,2,0:T(4,128)(2,1)}, u32[]{:S(2)}) copy-start(bf16[1,4,1,256,256]{4,1,3,2,0:T(4,128)(2,1)} %copy.61) | copy-start | bytes 1572868
  190.8 3.3 %copy-start.5 = (bf16[128,4,2,1792]{0,3,1,2:T(8,128)(2,1)S(1)}, bf16[128,4,2,1792]{0,3,1,2:T(8,128)(2,1)}, u32[]{:S(2)}) copy-start(bf16[128,4,2,1792]{0,3,1,2:T(8,128)(2,1)} %constant_dynamic-update-slice_fusion.3) | copy-start | bytes 11010052
Sparse Core Ops, SparseCore 0:
  10.1 84.9 all-gather.1
